TPU v7x, 32 devices: a whole 2x2x4 slice. The times are simulated.
32 devices in a mesh: wrap: 8 (over z, y), samp: 4 (over x, core).
Axes of the slice: x: 2, y: 2, z: 4, core: 2. Of those that a mesh axis runs over, the one named last changes fastest.
Arguments:
- inputs: bfloat16 [4, 64, 64, 256], P('samp', None, 'wrap'), may hold values from -6 to 6
- cotangent: bfloat16 [4, 64, 64, 256], P('samp', None, 'wrap'), may hold values from -6 to 6
- weight_one: bfloat16 [64, 1728], replicated, may hold values from -0.15625 to 0.15625
- bias_one: float32 [64], replicated, may hold values from -3 to 3
- weight_two: bfloat16 [64, 1728], replicated, may hold values from -0.15625 to 0.15625
- bias_two: float32 [64], replicated, may hold values from -3 to 3
- dilation: int32 [2], replicated, may hold values from 1 to 4, as said below
Outputs:
- prediction: bfloat16 [4, 64, 64, 256], P('samp', None, 'wrap')
- grad_weight_one: float32 [64, 1728], replicated
- grad_bias_one: float32 [64], replicated
- grad_weight_two: float32 [64, 1728], replicated
- grad_bias_two: float32 [64], replicated
Inputs may be any that keep to these rules, and one draw needn't show every extreme that they name: `dilation`: in every draw one of the two rates equals 4.
All inputs are finite; a program needn't handle non-finite values.
Results may differ from a plain program's by a relative error of at most 0.006.
Values may be sent and summed in bfloat16 or wider, within the bound.
No kernel may reach another device: no remote copies, remote signals or barrier semaphores. Data moves between devices by JAX's collectives and lax.ppermute only.
A program may use at most 128 MiB of HBM per device.

v0:
```python
import math
import jax
import jax.numpy as jnp
from jax import lax
from jax.sharding import PartitionSpec as P

DMAX = 4
NR = 16
S = 16


def with_halo(x, sides, width):
    for axis, dim in sides:
        size, length = (lax.axis_size(axis), x.shape[dim])
        up = [(i, (i + 1) % size) for i in range(size)]
        down = [(j, i) for i, j in up]
        last = lax.slice_in_dim(x, length - width, length, axis=dim)
        initial = lax.slice_in_dim(x, 0, width, axis=dim)
        before = lax.ppermute(last, axis, up)
        after = lax.ppermute(initial, axis, down)
        x = jnp.concatenate([before, x, after], axis=dim)
    return x


def grid_of(field):
    chans = field.shape[0]
    shaped = field.reshape(chans, field.shape[1], NR, S)
    return jnp.pad(shaped, ((0, 0), (0, 0), (DMAX, DMAX), (DMAX, DMAX)))


def tap_stack(padded, rate, first_row, out_rows, tap_w):
    in_chan = padded.shape[0]
    anchor = jnp.zeros((), jnp.int32)
    windows = []
    for tap_n in range(3):
        for tap_s in range(3):
            offsets = (
                anchor,
                first_row + (tap_w - 1) * rate,
                DMAX + (tap_n - 1) * rate,
                DMAX + (tap_s - 1) * rate,
            )
            window = lax.dynamic_slice(padded, offsets, (in_chan, out_rows, NR, S))
            windows.append(window.reshape(in_chan, -1))
    return jnp.concatenate(windows, 0)


def convolve(padded, weight, rate, first_row, out_rows):
    in_chan = padded.shape[0]
    summed = None
    for tap_w in range(3):
        stacked = tap_stack(padded, rate, first_row, out_rows, tap_w)
        term = jnp.dot(
            weight[:, tap_w * 9 * in_chan : (tap_w + 1) * 9 * in_chan],
            stacked,
            preferred_element_type=jnp.float32,
        )
        summed = term if summed is None else summed + term
    return summed


def weight_grad(cot, padded, rate, first_row, out_rows):
    columns = []
    for tap_w in range(3):
        stacked = tap_stack(padded, rate, first_row, out_rows, tap_w)
        columns.append(
            lax.dot_general(
                cot, stacked, (((1,), (1,)), ((), ())), preferred_element_type=jnp.float32
            )
        )
    return jnp.concatenate(columns, 1)


def flip_kernel(weight):
    chans = weight.shape[0]
    shaped = weight.reshape(chans, 27, chans)[:, ::-1, :]
    return jnp.transpose(shaped, (2, 1, 0)).reshape(chans, 27 * chans)


def body(inputs, cotangent, weight_one, bias_one, weight_two, bias_two, dilation):
    samples_here = inputs.shape[0]
    chans = inputs.shape[1]
    rows = inputs.shape[2]
    first_rate = dilation[0]
    second_rate = dilation[1]
    factor = 1.0 / math.sqrt(
        samples_here * lax.axis_size("samp") * rows * lax.axis_size("wrap") * inputs.shape[3]
    )
    flipped = flip_kernel(weight_two)
    extended = with_halo(inputs, (("wrap", 2),), DMAX)
    sample = 0
    grid_in = grid_of(extended[sample])
    pre_one = convolve(grid_in, weight_one, first_rate, DMAX, rows) + bias_one[:, None]
    pre_list = [pre_one]
    hidden_list = [jax.nn.silu(pre_one).astype(jnp.bfloat16).reshape(chans, rows, -1)]
    grids = [grid_in]
    hidden_ext = with_halo(jnp.stack(hidden_list), (("wrap", 2),), DMAX)
    sample = 0
    hidden_grids = [grid_of(hidden_ext[sample])]
    input_first = DMAX
    grad_two = None
    bias_two_grad = None
    sample = 0
    output = (
        convolve(hidden_grids[sample], weight_two, second_rate, DMAX, rows) + bias_two[:, None]
    ).astype(jnp.bfloat16)
    outputs = [output.reshape(chans, rows, -1)]
    cot_flat = cotangent[sample].reshape(chans, -1)
    term = weight_grad(cot_flat, hidden_grids[sample], second_rate, DMAX, rows)
    bias_term = jnp.sum(cot_flat.astype(jnp.float32), 1)
    grad_two = term
    bias_two_grad = bias_term
    grad_two = grad_two * factor
    bias_two_grad = bias_two_grad * factor
    cot_ext = with_halo(cotangent, (("wrap", 2),), DMAX)
    grad_one = None
    bias_one_grad = None
    sample = 0
    back_hidden = convolve(grid_of(cot_ext[sample]), flipped, second_rate, DMAX, rows)
    pre_one = pre_list[sample]
    sigm = jax.nn.sigmoid(pre_one)
    back_pre = (back_hidden * sigm * (1.0 + pre_one * (1.0 - sigm))).astype(jnp.bfloat16)
    term = weight_grad(back_pre, grids[sample], first_rate, input_first, rows)
    bias_term = jnp.sum(back_pre.astype(jnp.float32), 1)
    grad_one = term
    bias_one_grad = bias_term
    grad_one = grad_one * factor
    bias_one_grad = bias_one_grad * factor
    grad_one, bias_one_grad, grad_two, bias_two_grad = lax.psum(
        (grad_one, bias_one_grad, grad_two, bias_two_grad), ("wrap", "samp")
    )
    return (jnp.stack(outputs), grad_one, bias_one_grad, grad_two, bias_two_grad)


def solution(mesh):
    in_specs = (
        P("samp", None, "wrap", None),
        P("samp", None, "wrap", None),
        P(),
        P(),
        P(),
        P(),
        P(),
    )
    out_specs = (P("samp", None, "wrap", None), P(), P(), P(), P())
    return jax.shard_map(body, mesh=mesh, in_specs=in_specs, out_specs=out_specs, check_vma=False)
```

profile of v0, /device:TPU:0, one launch (start us, length us, event | category | flops | bytes accessed | tf_op | source)
XLA Modules:
  0.0 347.6 jit_solution(2324225012075709310)
XLA Ops:
  9.3 3.0 collective-permute-start.4
  12.3 3.0 collective-permute-start.5
  16.8 4.7 %collective-permute-start.1 = (bf16[1,64,4,256]{1,3,2,0:T(8,128)(2,1)S(1)}, bf16[1,64,4,256]{1,3,2,0:T(8,128)(2,1)}, u32[]{:S(2)}, u32[]{:S(2)}) collective-permute-start(bf16[1,64,4,256]{1,3,2,0:T(8,128)(2,1)S(1)} %get-tuple-element.94), channel_id=1, source_target_pairs={{4,0},{8,4},{12,8},{16,12},{20,16},{24,20},{28,24},{0,28},{5,1},{9... | collective-permute-start | bytes 393224 | tf_op jit(solution)/shard_map/ppermute | solution.py:20
  34.1 4.6 %pad_dynamic-slice_fusion = (bf16[64,8,16,16]{0,3,2,1:T(8,128)(2,1)}, bf16[64,8,16,16]{0,3,2,1:T(8,128)(2,1)}, bf16[64,8,16,16]{0,3,2,1:T(8,128)(2,1)}, bf16[64,...) fusion(s32[]{:T(128)S(6)} %select_n.23, ...), kind=kLoop, calls=%fused_computation | loop fusion | bytes 5505040 | tf_op jit(solution)/shard_map/dynamic_slice | solution.py:43
  38.7 4.6 %pad_dynamic-slice_fusion.1 = (bf16[64,8,16,16]{0,3,2,1:T(8,128)(2,1)}, bf16[64,8,16,16]{0,3,2,1:T(8,128)(2,1)}, bf16[64,8,16,16]{0,3,2,1:T(8,128)(2,1)}, bf16[6...) fusion(s32[]{:T(128)S(6)} %select_n.23, ...), kind=kLoop, calls=%fused_computation.1 | loop fusion | bytes 3670032 | tf_op jit(solution)/shard_map/dynamic_slice | solution.py:43
  44.6 4.6 %pad_dynamic-slice_fusion.26 = (bf16[64,8,16,16]{0,3,2,1:T(8,128)(2,1)}, bf16[64,8,16,16]{0,3,2,1:T(8,128)(2,1)}, bf16[64,8,16,16]{0,3,2,1:T(8,128)(2,1)}, bf16[...) fusion(s32[]{:T(128)S(6)} %select_n.19, ...), kind=kLoop, calls=%fused_computation.26 | loop fusion | bytes 5505040 | tf_op jit(solution)/shard_map/dynamic_slice | solution.py:43
  49.2 4.6 %pad_dynamic-slice_fusion.27 = (bf16[64,8,16,16]{0,3,2,1:T(8,128)(2,1)}, bf16[64,8,16,16]{0,3,2,1:T(8,128)(2,1)}, bf16[64,8,16,16]{0,3,2,1:T(8,128)(2,1)}, bf16[...) fusion(s32[]{:T(128)S(6)} %select_n.19, ...), kind=kLoop, calls=%fused_computation.27 | loop fusion | bytes 3670032 | tf_op jit(solution)/shard_map/dynamic_slice | solution.py:43
  53.8 5.2 %concatenate.67 = bf16[576,2048]{0,1:T(8,128)(2,1)S(1)} concatenate(bf16[64,2048]{0,1:T(8,128)(2,1)} %bitcast.166, bf16[64,2048]{0,1:T(8,128)(2,1)S(1)} %bitcast.163, bf16[64,2048]{0,1:T(8,128)(2,1)} %bitcast.212, bf16[64,2048]{0,1:T(8,128)(2,1)} %bitcast.164, bf16[64,2048]{0,1:T(8,128)(2,1)} %bitcast.165, bf16[64,2048]{0,1:T(8,128)(2,1)} %bitcast.211, ...), dimensions={0} | concatenate | bytes 4718592 | tf_op jit(solution)/shard_map/concatenate | solution.py:45
  60.8 5.5 %concatenate.68 = bf16[576,2048]{0,1:T(8,128)(2,1)S(1)} concatenate(bf16[64,2048]{0,1:T(8,128)(2,1)} %bitcast.154, bf16[64,2048]{0,1:T(8,128)(2,1)} %bitcast.155, bf16[64,2048]{0,1:T(8,128)(2,1)} %bitcast.162, bf16[64,2048]{0,1:T(8,128)(2,1)} %bitcast.156, bf16[64,2048]{0,1:T(8,128)(2,1)} %bitcast.157, bf16[64,2048]{0,1:T(8,128)(2,1)} %bitcast.161, bf16[64,2048]{0,1:T(8,128)(2,1)} %bitcast.160, ...), dimensions={0} | concatenate | bytes 4718592 | tf_op jit(solution)/shard_map/concatenate | solution.py:45
  66.3 2.6 convolution_add_fusion.2
  69.0 5.3 %concatenate.56 = bf16[576,2048]{0,1:T(8,128)(2,1)S(1)} concatenate(bf16[64,2048]{0,1:T(8,128)(2,1)} %bitcast.190, bf16[64,2048]{0,1:T(8,128)(2,1)} %bitcast.187, bf16[64,2048]{0,1:T(8,128)(2,1)} %bitcast.224, bf16[64,2048]{0,1:T(8,128)(2,1)} %bitcast.188, bf16[64,2048]{0,1:T(8,128)(2,1)} %bitcast.189, bf16[64,2048]{0,1:T(8,128)(2,1)} %bitcast.223, bf16[64,2048]{0,1:T(8,128)(2,1)} %bitcast.222, ...), dimensions={0} | concatenate | bytes 4718592 | tf_op jit(solution)/shard_map/concatenate | solution.py:45
  76.1 6.8 %concatenate.57 = bf16[576,2048]{0,1:T(8,128)(2,1)} concatenate(bf16[64,2048]{0,1:T(8,128)(2,1)} %bitcast.178, bf16[64,2048]{0,1:T(8,128)(2,1)} %bitcast.179, bf16[64,2048]{0,1:T(8,128)(2,1)} %bitcast.186, bf16[64,2048]{0,1:T(8,128)(2,1)} %bitcast.180, bf16[64,2048]{0,1:T(8,128)(2,1)} %bitcast.181, bf16[64,2048]{0,1:T(8,128)(2,1)} %bitcast.185, bf16[64,2048]{0,1:T(8,128)(2,1)} %bitcast.184, ...), dimensions={0} | concatenate | bytes 4718592 | tf_op jit(solution)/shard_map/concatenate | solution.py:45
  82.9 3.5 %convolution_add_fusion.4 = f32[2048,64]{0,1:T(8,128)} fusion(f32[2048,64]{0,1:T(8,128)S(1)} %fusion.26, bf16[576,2048]{0,1:T(8,128)(2,1)} %concatenate.57, bf16[64,1728]{1,0:T(8,128)(2,1)} %param.9), kind=kOutput, calls=%fused_computation.75 | convolution fusion | flops 151126016 | bytes 3751936 | tf_op jit(solution)/shard_map/dot_general | solution.py:53
  86.4 6.8 %concatenate.58 = bf16[576,2048]{0,1:T(8,128)(2,1)} concatenate(bf16[64,2048]{0,1:T(8,128)(2,1)} %bitcast.220, bf16[64,2048]{0,1:T(8,128)(2,1)} %bitcast.219, bf16[64,2048]{0,1:T(8,128)(2,1)} %bitcast.218, bf16[64,2048]{0,1:T(8,128)(2,1)} %bitcast.217, bf16[64,2048]{0,1:T(8,128)(2,1)} %bitcast.216, bf16[64,2048]{0,1:T(8,128)(2,1)} %bitcast.215, bf16[64,2048]{0,1:T(8,128)(2,1)} %bitcast.214, ...), dimensions={0} | concatenate | bytes 4718592 | tf_op jit(solution)/shard_map/concatenate | solution.py:45
  93.3 3.7 %multiply_convert_fusion = (bf16[64,2048]{1,0:T(8,128)(2,1)}, f32[64,2048]{1,0:T(8,128)}) fusion(f32[64]{0:T(128)S(1)} %copy-done.17, f32[2048,64]{0,1:T(8,128)} %convolution_add_fusion.4, bf16[576,2048]{0,1:T(8,128)(2,1)} %concatenate.58, bf16[64,1728]{1,0:T(8,128)(2,1)} %param.9), kind=kOutput, calls=%fused_computation.85 | convolution fusion | flops 151912448 | bytes 4014336 | tf_op jit(solution)/shard_map/dot_general | solution.py:53
  97.0 6.7 %concatenate.69 = bf16[576,2048]{0,1:T(8,128)(2,1)} concatenate(bf16[64,2048]{0,1:T(8,128)(2,1)} %bitcast.208, bf16[64,2048]{0,1:T(8,128)(2,1)} %bitcast.207, bf16[64,2048]{0,1:T(8,128)(2,1)} %bitcast.206, bf16[64,2048]{0,1:T(8,128)(2,1)} %bitcast.205, bf16[64,2048]{0,1:T(8,128)(2,1)} %bitcast.204, bf16[64,2048]{0,1:T(8,128)(2,1)} %bitcast.203, bf16[64,2048]{0,1:T(8,128)(2,1)} %bitcast.202, ...), dimensions={0} | concatenate | bytes 4718592 | tf_op jit(solution)/shard_map/concatenate | solution.py:45
  103.7 3.2 convert_reduce_fusion.1
  111.7 4.5 %collective-permute-start.3 = (bf16[1,64,4,256]{1,3,2,0:T(8,128)(2,1)S(1)}, bf16[1,64,4,256]{1,3,2,0:T(8,128)(2,1)S(1)}, u32[]{:S(2)}, u32[]{:S(2)}) collective-permute-start(bf16[1,64,4,256]{1,3,2,0:T(8,128)(2,1)S(1)} %get-tuple-element.92), channel_id=1, source_target_pairs={{4,0},{8,4},{12,8},{16,12},{20,16},{24,20},{28,24},{0,28},{5,1},{9... | collective-permute-start | bytes 393224 | tf_op jit(solution)/shard_map/ppermute | solution.py:20
  118.0 40.3 %all-reduce.3 = (f32[64]{0:T(128)}, f32[64]{0:T(128)}) all-reduce(f32[64]{0:T(128)S(1)} %broadcast_multiply_fusion.3, f32[64]{0:T(128)S(1)} %broadcast_multiply_fusion.2), channel_id=1, replica_groups=mesh['wrap'=8,'samp'=4] {'wrap','samp'}, use_global_device_ids=true, to_apply=%region_2.3 | all-reduce | flops 128 | bytes 1024 | tf_op jit(solution)/shard_map/psum | solution.py:129
  158.4 2.6 select_maximum_fusion
  161.0 7.1 %constant_dynamic-slice_fusion.9 = (bf16[64,8,16,16]{0,3,2,1:T(8,128)(2,1)S(1)}, bf16[64,8,16,16]{0,3,2,1:T(8,128)(2,1)}, bf16[64,8,16,16]{0,3,2,1:T(8,128)(2,1)...) fusion(bf16[64,16,24,24]{0,3,2,1:T(8,128)(2,1)S(1)} %select_max, ...), kind=kLoop, calls=%fused_computation.120 | loop fusion | bytes 13631504 | tf_op jit(solution)/shard_map/dynamic_slice | solution.py:43
  185.9 5.3 %concatenate.63 = bf16[576,2048]{0,1:T(8,128)(2,1)S(1)} concatenate(bf16[64,2048]{0,1:T(8,128)(2,1)} %bitcast.200, bf16[64,2048]{0,1:T(8,128)(2,1)} %bitcast.199, bf16[64,2048]{0,1:T(8,128)(2,1)} %bitcast.198, bf16[64,2048]{0,1:T(8,128)(2,1)} %bitcast.197, bf16[64,2048]{0,1:T(8,128)(2,1)} %bitcast.196, bf16[64,2048]{0,1:T(8,128)(2,1)} %bitcast.195, bf16[64,2048]{0,1:T(8,128)(2,1)} %bitcast.194, ...), dimensions={0} | concatenate | bytes 4718592 | tf_op jit(solution)/shard_map/concatenate | solution.py:45
  196.5 5.3 %concatenate.65 = bf16[576,2048]{0,1:T(8,128)(2,1)S(1)} concatenate(bf16[64,2048]{0,1:T(8,128)(2,1)} %bitcast.175, bf16[64,2048]{0,1:T(8,128)(2,1)} %bitcast.174, bf16[64,2048]{0,1:T(8,128)(2,1)} %bitcast.173, bf16[64,2048]{0,1:T(8,128)(2,1)} %bitcast.172, bf16[64,2048]{0,1:T(8,128)(2,1)} %bitcast.171, bf16[64,2048]{0,1:T(8,128)(2,1)} %bitcast.170, bf16[64,2048]{0,1:T(8,128)(2,1)} %bitcast.169, ...), dimensions={0} | concatenate | bytes 4718592 | tf_op jit(solution)/shard_map/concatenate | solution.py:45
  211.4 125.7 %all-reduce.7.cloned.1.call-done = (f32[64,1728]{1,0:T(8,128)}, f32[64,1728]{1,0:T(8,128)}) async-done(((f32[64,1728]{1,0:T(8,128)}, f32[64,1728]{1,0:T(8,128)}), (f32[64,1728]{1,0:T(8,128)}, f32[64,1728]{1,0:T(8,128)})) %all-reduce.7.cloned.1.call-update) | async-done | bytes 884752 | tf_op jit(solution)/shard_map/psum | solution.py:129
  (97 shorter events, 58.4 us)
Async XLA Ops:
  7.2 20.1 %copy-start.6 = (bf16[1,64,8,256]{3,2,1,0:T(8,128)(2,1)S(1)}, bf16[1,64,8,256]{3,2,1,0:T(8,128)(2,1)}, u32[]{:S(2)}) copy-start(bf16[1,64,8,256]{3,2,1,0:T(8,128)(2,1)} %param.8) | copy-start | bytes 786436
  7.2 14.3 %copy-start.15 = (s32[2]{0:T(128)S(1)}, s32[2]{0:T(128)}, u32[]{:S(2)}) copy-start(s32[2]{0:T(128)} %param.13) | copy-start | bytes 28
  7.2 20.6 %copy-start.14 = (bf16[64,1728]{1,0:T(8,128)(2,1)S(1)}, bf16[64,1728]{1,0:T(8,128)(2,1)}, u32[]{:S(2)}) copy-start(bf16[64,1728]{1,0:T(8,128)(2,1)} %param.11) | copy-start | bytes 663556
  7.2 329.9 %all-reduce.7.cloned.1.call-start = ((), (), s32[]{:S(2)}) async-start(), calls=%async_computation | async-start | bytes 1835008 | tf_op jit(solution)/shard_map/psum | solution.py:129
  9.3 21.8 %collective-permute-start.4 = (bf16[1,64,4,256]{1,3,2,0:T(8,128)(2,1)}, bf16[1,64,4,256]{1,3,2,0:T(8,128)(2,1)}, u32[]{:S(2)}, u32[]{:S(2)}) collective-permute-start(bf16[1,64,4,256]{1,3,2,0:T(8,128)(2,1)} %get-tuple-element.89), channel_id=1, source_target_pairs={{0,4},{4,8},{8,12},{12,16},{16,20},{20,24},{24,28},{28,0},{1,5},{5... | collective-permute-start | bytes 393224 | tf_op jit(solution)/shard_map/ppermute | solution.py:19
  12.3 20.5 %collective-permute-start.5 = (bf16[1,64,4,256]{1,3,2,0:T(8,128)(2,1)S(1)}, bf16[1,64,4,256]{1,3,2,0:T(8,128)(2,1)}, u32[]{:S(2)}, u32[]{:S(2)}) collective-permute-start(bf16[1,64,4,256]{1,3,2,0:T(8,128)(2,1)S(1)} %get-tuple-element.90), channel_id=1, source_target_pairs={{4,0},{8,4},{12,8},{16,12},{20,16},{24,20},{28,24},{0,28},{5,1},{9... | collective-permute-start | bytes 393224 | tf_op jit(solution)/shard_map/ppermute | solution.py:20
  16.7 26.6 %collective-permute-start = (bf16[1,64,4,256]{1,3,2,0:T(8,128)(2,1)S(1)}, bf16[1,64,4,256]{1,3,2,0:T(8,128)(2,1)}, u32[]{:S(2)}, u32[]{:S(2)}) collective-permute-start(bf16[1,64,4,256]{1,3,2,0:T(8,128)(2,1)S(1)} %get-tuple-element.93), channel_id=1, source_target_pairs={{0,4},{4,8},{8,12},{12,16},{16,20},{20,24},{24,28},{28,0},{1,5},{5... | collective-permute-start | bytes 393224 | tf_op jit(solution)/shard_map/ppermute | solution.py:19
  16.8 26.6 %collective-permute-start.1 = (bf16[1,64,4,256]{1,3,2,0:T(8,128)(2,1)S(1)}, bf16[1,64,4,256]{1,3,2,0:T(8,128)(2,1)}, u32[]{:S(2)}, u32[]{:S(2)}) collective-permute-start(bf16[1,64,4,256]{1,3,2,0:T(8,128)(2,1)S(1)} %get-tuple-element.94), channel_id=1, source_target_pairs={{4,0},{8,4},{12,8},{16,12},{20,16},{24,20},{28,24},{0,28},{5,1},{9... | collective-permute-start | bytes 393224 | tf_op jit(solution)/shard_map/ppermute | solution.py:20
  49.2 4.6 %copy-start.8 = (bf16[64,8,16,16]{0,3,2,1:T(8,128)(2,1)S(1)}, bf16[64,8,16,16]{0,3,2,1:T(8,128)(2,1)}, u32[]{:S(2)}) copy-start(bf16[64,8,16,16]{0,3,2,1:T(8,128)(2,1)} %get-tuple-element.36) | copy-start | bytes 786436
  86.4 6.8 %copy-start.17 = (f32[64]{0:T(128)S(1)}, f32[64]{0:T(128)}, u32[]{:S(2)}) copy-start(f32[64]{0:T(128)} %param.10) | copy-start | bytes 772
  93.2 3.8 %copy-start.7 = (bf16[64,8,16,16]{0,3,2,1:T(8,128)(2,1)S(1)}, bf16[64,8,16,16]{0,3,2,1:T(8,128)(2,1)}, u32[]{:S(2)}) copy-start(bf16[64,8,16,16]{0,3,2,1:T(8,128)(2,1)} %get-tuple-element.35) | copy-start | bytes 786436
  103.7 3.2 copy-start.5
  106.9 1.8 copy-start
  108.6 2.4 copy-start.9
  111.4 47.0 %collective-permute-start.2 = (bf16[1,64,4,256]{1,3,2,0:T(8,128)(2,1)S(1)}, bf16[1,64,4,256]{1,3,2,0:T(8,128)(2,1)S(1)}, u32[]{:S(2)}, u32[]{:S(2)}) collective-permute-start(bf16[1,64,4,256]{1,3,2,0:T(8,128)(2,1)S(1)} %get-tuple-element.91), channel_id=1, source_target_pairs={{0,4},{4,8},{8,12},{12,16},{16,20},{20,24},{24,28},{28,0},{1,5},{5... | collective-permute-start | bytes 393224 | tf_op jit(solution)/shard_map/ppermute | solution.py:19
  111.7 46.7 %collective-permute-start.3 = (bf16[1,64,4,256]{1,3,2,0:T(8,128)(2,1)S(1)}, bf16[1,64,4,256]{1,3,2,0:T(8,128)(2,1)S(1)}, u32[]{:S(2)}, u32[]{:S(2)}) collective-permute-start(bf16[1,64,4,256]{1,3,2,0:T(8,128)(2,1)S(1)} %get-tuple-element.92), channel_id=1, source_target_pairs={{4,0},{8,4},{12,8},{16,12},{20,16},{24,20},{28,24},{0,28},{5,1},{9... | collective-permute-start | bytes 393224 | tf_op jit(solution)/shard_map/ppermute | solution.py:20
  178.8 7.1 %copy-start.1 = (bf16[576,2048]{1,0:T(8,128)(2,1)}, bf16[576,2048]{1,0:T(8,128)(2,1)S(1)}, u32[]{:S(2)}) copy-start(bf16[576,2048]{1,0:T(8,128)(2,1)S(1)} %constant_dynamic-update-slice_fusion.4) | copy-start | bytes 7077892
  191.2 3.1 copy-start.12
  193.1 1.7 copy-start.2
  193.1 1.7 copy-start.13
  193.1 1.8 copy-start.11
  193.1 1.8 copy-start.10
  207.1 2.0 copy-start.4
  207.1 2.0 copy-start.16
  (1 other events, 1.5 us)
Sparse Core Ops, SparseCore 0:
  207.3 129.7 all-reduce.6
where the time goes:
time: 351 us; the launch traced here: 348 us
  waiting for transfers between devices  127 us (36%)
  local copies, waits for them, and re-layouts  108 us (31%)
  blocking collectives  40.3 us (11%)
  matrix products  28.9 us (8%)
  between operations  19.6 us (6%)
  starting transfers between devices  15.6 us (4%)
  other arithmetic  7.83 us (2%)
    psum x1, waiting for transfers between devices, body(): lax.psum((grad_one, bias_one_grad, grad_two, bias_two_grad), ('wrap', 'sa...  126 us
    concatenate x9, local copies, waits for them, and re-layouts, tap_stack(): return jnp.concatenate(windows, 0)  47 us
    psum x1, blocking collectives, body(): lax.psum((grad_one, bias_one_grad, grad_two, bias_two_grad), ('wrap', 'sa...  40.3 us
    dynamic_slice x5, local copies, waits for them, and re-layouts, tap_stack(): window = lax.dynamic_slice(padded, offsets, (in_chan, out_rows, NR, S))  25.5 us
    dot_general x9, matrix products, convolve(): jnp.dot(weight[:, tap_w * 9 * in_chan:(tap_w + 1) * 9 * in_chan], stacked...  22 us
    reshape x8, local copies, waits for them, and re-layouts, tap_stack(): windows.append(window.reshape(in_chan, -1))  13.8 us
    unnamed x50, local copies, waits for them, and re-layouts  12.8 us
    ppermute x3, starting transfers between devices, with_halo(): after = lax.ppermute(initial, axis, down)  12.3 us
  transfers between devices with their start and end apart: 7, of which 2 were waited for; matrix products, arithmetic and copies ran while one was open for 6% of the time, Pallas kernels for 0%

commit v1 on v0

--- a/solution.py
+++ b/solution.py
@@ -7,6 +7,11 @@
 DMAX = 4
 NR = 16
 S = 16
+
+
+def one_after_other(value, one, other):
+    inner = lax.psum(value, one)
+    return lax.psum(inner, other)
 
 
 def with_halo(x, sides, width):
@@ -126,8 +131,8 @@
     bias_one_grad = bias_term
     grad_one = grad_one * factor
     bias_one_grad = bias_one_grad * factor
-    grad_one, bias_one_grad, grad_two, bias_two_grad = lax.psum(
-        (grad_one, bias_one_grad, grad_two, bias_two_grad), ("wrap", "samp")
+    grad_one, bias_one_grad, grad_two, bias_two_grad = one_after_other(
+        (grad_one, bias_one_grad, grad_two, bias_two_grad), "wrap", "samp"
     )
     return (jnp.stack(outputs), grad_one, bias_one_grad, grad_two, bias_two_grad)
 

time: 351 us -> 302 us (0.86)
  waiting for transfers between devices: 127 us -> 87.2 us
  blocking collectives: 40.3 us -> 25.9 us
  local copies, waits for them, and re-layouts: 108 us -> 112 us
    psum x1 -> x2, waiting for transfers between devices: 126 us -> 81.1 us  [the longest x1 47 us: one_after_other(): inner = lax.psum(value, one)]
    psum x1 -> x2, blocking collectives: 40.3 us -> 25.9 us  [the longest x1 19.8 us: one_after_other(): inner = lax.psum(value, one)]
    unnamed x50 -> x44, local copies, waits for them, and re-layouts: 12.8 us -> 15.3 us
  transfers between devices with their start and end apart: 7 -> 8, of which waited for: 2 -> 5; matrix products, arithmetic and copies ran while one was open for 6% -> 9% of each run, Pallas kernels for 0% -> 0%
where the time goes in v1:
time: 302 us; the launch traced here: 298 us
  local copies, waits for them, and re-layouts  112 us (37%)
  waiting for transfers between devices  87.2 us (29%)
  matrix products  29.6 us (10%)
  blocking collectives  25.9 us (9%)
  between operations  19.6 us (6%)
  starting transfers between devices  15.7 us (5%)
  other arithmetic  8.32 us (3%)
    psum x1, waiting for transfers between devices, one_after_other(): inner = lax.psum(value, one)  47 us
    concatenate x9, local copies, waits for them, and re-layouts, tap_stack(): return jnp.concatenate(windows, 0)  46.9 us
    psum x1, waiting for transfers between devices, one_after_other(): return lax.psum(inner, other)  34 us
    dynamic_slice x5, local copies, waits for them, and re-layouts, tap_stack(): window = lax.dynamic_slice(padded, offsets, (in_chan, out_rows, NR, S))  25.3 us
    dot_general x9, matrix products, convolve(): jnp.dot(weight[:, tap_w * 9 * in_chan:(tap_w + 1) * 9 * in_chan], stacked...  20.9 us
    psum x1, blocking collectives, one_after_other(): inner = lax.psum(value, one)  19.8 us
    unnamed x44, local copies, waits for them, and re-layouts  15.3 us
    reshape x8, local copies, waits for them, and re-layouts, tap_stack(): windows.append(window.reshape(in_chan, -1))  14.7 us
  transfers between devices with their start and end apart: 8, of which 5 were waited for; matrix products, arithmetic and copies ran while one was open for 9% of the time, Pallas kernels for 0%

profile of v1, /device:TPU:0, one launch (start us, length us, event | category | flops | bytes accessed | tf_op | source)
XLA Modules:
  0.0 298.4 jit_solution(1199023042302809043)
XLA Ops:
  16.9 4.7 %collective-permute-start.1 = (bf16[1,64,4,256]{1,3,2,0:T(8,128)(2,1)}, bf16[1,64,4,256]{1,3,2,0:T(8,128)(2,1)}, u32[]{:S(2)}, u32[]{:S(2)}) collective-permute-start(bf16[1,64,4,256]{1,3,2,0:T(8,128)(2,1)} %get-tuple-element.98), channel_id=1, source_target_pairs={{4,0},{8,4},{12,8},{16,12},{20,16},{24,20},{28,24},{0,28},{5,1},{9... | collective-permute-start | bytes 393224 | tf_op jit(solution)/shard_map/ppermute | solution.py:25
  33.4 4.7 %pad_dynamic-slice_fusion = (bf16[64,8,16,16]{0,3,2,1:T(8,128)(2,1)}, bf16[64,8,16,16]{0,3,2,1:T(8,128)(2,1)S(1)}, bf16[64,8,16,16]{0,3,2,1:T(8,128)(2,1)}, bf16...) fusion(s32[]{:T(128)S(6)} %select_n.23, ...), kind=kLoop, calls=%fused_computation | loop fusion | bytes 5505040 | tf_op jit(solution)/shard_map/dynamic_slice | solution.py:48
  38.2 4.5 %pad_dynamic-slice_fusion.1 = (bf16[64,8,16,16]{0,3,2,1:T(8,128)(2,1)}, bf16[64,8,16,16]{0,3,2,1:T(8,128)(2,1)}, bf16[64,8,16,16]{0,3,2,1:T(8,128)(2,1)}, bf16[6...) fusion(s32[]{:T(128)S(6)} %select_n.23, ...), kind=kLoop, calls=%fused_computation.1 | loop fusion | bytes 3670032 | tf_op jit(solution)/shard_map/dynamic_slice | solution.py:48
  43.9 4.6 %pad_dynamic-slice_fusion.26 = (bf16[64,8,16,16]{0,3,2,1:T(8,128)(2,1)}, bf16[64,8,16,16]{0,3,2,1:T(8,128)(2,1)}, bf16[64,8,16,16]{0,3,2,1:T(8,128)(2,1)}, bf16[...) fusion(s32[]{:T(128)S(6)} %select_n.19, ...), kind=kLoop, calls=%fused_computation.26 | loop fusion | bytes 5505040 | tf_op jit(solution)/shard_map/dynamic_slice | solution.py:48
  48.5 4.5 %pad_dynamic-slice_fusion.27 = (bf16[64,8,16,16]{0,3,2,1:T(8,128)(2,1)}, bf16[64,8,16,16]{0,3,2,1:T(8,128)(2,1)}, bf16[64,8,16,16]{0,3,2,1:T(8,128)(2,1)}, bf16[...) fusion(s32[]{:T(128)S(6)} %select_n.19, ...), kind=kLoop, calls=%fused_computation.27 | loop fusion | bytes 3670032 | tf_op jit(solution)/shard_map/dynamic_slice | solution.py:48
  53.0 5.2 %concatenate.67 = bf16[576,2048]{0,1:T(8,128)(2,1)S(1)} concatenate(bf16[64,2048]{0,1:T(8,128)(2,1)} %bitcast.166, bf16[64,2048]{0,1:T(8,128)(2,1)S(1)} %bitcast.163, bf16[64,2048]{0,1:T(8,128)(2,1)} %bitcast.212, bf16[64,2048]{0,1:T(8,128)(2,1)} %bitcast.164, bf16[64,2048]{0,1:T(8,128)(2,1)} %bitcast.165, bf16[64,2048]{0,1:T(8,128)(2,1)} %bitcast.211, ...), dimensions={0} | concatenate | bytes 4718592 | tf_op jit(solution)/shard_map/concatenate | solution.py:50
  60.1 5.5 %concatenate.68 = bf16[576,2048]{0,1:T(8,128)(2,1)S(1)} concatenate(bf16[64,2048]{0,1:T(8,128)(2,1)} %bitcast.154, bf16[64,2048]{0,1:T(8,128)(2,1)} %bitcast.155, bf16[64,2048]{0,1:T(8,128)(2,1)} %bitcast.162, bf16[64,2048]{0,1:T(8,128)(2,1)} %bitcast.156, bf16[64,2048]{0,1:T(8,128)(2,1)} %bitcast.157, bf16[64,2048]{0,1:T(8,128)(2,1)} %bitcast.161, bf16[64,2048]{0,1:T(8,128)(2,1)} %bitcast.160, ...), dimensions={0} | concatenate | bytes 4718592 | tf_op jit(solution)/shard_map/concatenate | solution.py:50
  68.2 5.3 %concatenate.56 = bf16[576,2048]{0,1:T(8,128)(2,1)S(1)} concatenate(bf16[64,2048]{0,1:T(8,128)(2,1)} %bitcast.199, bf16[64,2048]{0,1:T(8,128)(2,1)} %bitcast.196, bf16[64,2048]{0,1:T(8,128)(2,1)} %bitcast.224, bf16[64,2048]{0,1:T(8,128)(2,1)} %bitcast.197, bf16[64,2048]{0,1:T(8,128)(2,1)} %bitcast.198, bf16[64,2048]{0,1:T(8,128)(2,1)} %bitcast.223, bf16[64,2048]{0,1:T(8,128)(2,1)} %bitcast.222, ...), dimensions={0} | concatenate | bytes 4718592 | tf_op jit(solution)/shard_map/concatenate | solution.py:50
  75.3 6.8 %concatenate.57 = bf16[576,2048]{0,1:T(8,128)(2,1)} concatenate(bf16[64,2048]{0,1:T(8,128)(2,1)} %bitcast.187, bf16[64,2048]{0,1:T(8,128)(2,1)} %bitcast.188, bf16[64,2048]{0,1:T(8,128)(2,1)} %bitcast.195, bf16[64,2048]{0,1:T(8,128)(2,1)} %bitcast.189, bf16[64,2048]{0,1:T(8,128)(2,1)} %bitcast.190, bf16[64,2048]{0,1:T(8,128)(2,1)} %bitcast.194, bf16[64,2048]{0,1:T(8,128)(2,1)} %bitcast.193, ...), dimensions={0} | concatenate | bytes 4718592 | tf_op jit(solution)/shard_map/concatenate | solution.py:50
  82.1 3.5 %convolution_add_fusion.4 = f32[2048,64]{0,1:T(8,128)} fusion(f32[2048,64]{0,1:T(8,128)S(1)} %fusion.26, bf16[576,2048]{0,1:T(8,128)(2,1)} %concatenate.57, bf16[64,1728]{1,0:T(8,128)(2,1)} %param.9), kind=kOutput, calls=%fused_computation.75 | convolution fusion | flops 151126016 | bytes 3751936 | tf_op jit(solution)/shard_map/dot_general | solution.py:58
  85.6 6.8 %concatenate.58 = bf16[576,2048]{0,1:T(8,128)(2,1)} concatenate(bf16[64,2048]{0,1:T(8,128)(2,1)} %bitcast.220, bf16[64,2048]{0,1:T(8,128)(2,1)} %bitcast.219, bf16[64,2048]{0,1:T(8,128)(2,1)} %bitcast.218, bf16[64,2048]{0,1:T(8,128)(2,1)} %bitcast.217, bf16[64,2048]{0,1:T(8,128)(2,1)} %bitcast.216, bf16[64,2048]{0,1:T(8,128)(2,1)} %bitcast.215, bf16[64,2048]{0,1:T(8,128)(2,1)} %bitcast.214, ...), dimensions={0} | concatenate | bytes 4718592 | tf_op jit(solution)/shard_map/concatenate | solution.py:50
  92.4 3.7 %multiply_convert_fusion = (bf16[64,2048]{1,0:T(8,128)(2,1)}, f32[64,2048]{1,0:T(8,128)}) fusion(f32[64]{0:T(128)S(1)} %copy-done.14, f32[2048,64]{0,1:T(8,128)} %convolution_add_fusion.4, bf16[576,2048]{0,1:T(8,128)(2,1)} %concatenate.58, bf16[64,1728]{1,0:T(8,128)(2,1)} %param.9), kind=kOutput, calls=%fused_computation.85 | convolution fusion | flops 151912448 | bytes 4014336 | tf_op jit(solution)/shard_map/dot_general | solution.py:58
  96.1 6.7 %concatenate.69 = bf16[576,2048]{0,1:T(8,128)(2,1)} concatenate(bf16[64,2048]{0,1:T(8,128)(2,1)} %bitcast.208, bf16[64,2048]{0,1:T(8,128)(2,1)} %bitcast.207, bf16[64,2048]{0,1:T(8,128)(2,1)} %bitcast.206, bf16[64,2048]{0,1:T(8,128)(2,1)} %bitcast.205, bf16[64,2048]{0,1:T(8,128)(2,1)} %bitcast.204, bf16[64,2048]{0,1:T(8,128)(2,1)} %bitcast.203, bf16[64,2048]{0,1:T(8,128)(2,1)} %bitcast.202, ...), dimensions={0} | concatenate | bytes 4718592 | tf_op jit(solution)/shard_map/concatenate | solution.py:50
  102.8 3.2 %convert_reduce_fusion.1 = (f32[64]{0:T(128)S(1)}, bf16[64,2048]{1,0:T(8,128)(2,1)S(1)}) fusion(f32[64,2048]{1,0:T(8,128)} %get-tuple-element.102, f32[2048,64]{0,1:T(8,128)} %convolution_add_fusion.2, bf16[576,2048]{0,1:T(8,128)(2,1)} %concatenate.69, bf16[64,1728]{1,0:T(8,128)(2,1)} %reshape.409), kind=kOutput, calls=%fused_computation.84 | convolution fusion | flops 152567744 | bytes 4014336 | tf_op jit(solution)/shard_map/dot_general | solution.py:58
  111.2 4.7 %collective-permute-start.3 = (bf16[1,64,4,256]{1,3,2,0:T(8,128)(2,1)}, bf16[1,64,4,256]{1,3,2,0:T(8,128)(2,1)}, u32[]{:S(2)}, u32[]{:S(2)}) collective-permute-start(bf16[1,64,4,256]{1,3,2,0:T(8,128)(2,1)} %get-tuple-element.96), channel_id=1, source_target_pairs={{4,0},{8,4},{12,8},{16,12},{20,16},{24,20},{28,24},{0,28},{5,1},{9... | collective-permute-start | bytes 393224 | tf_op jit(solution)/shard_map/ppermute | solution.py:25
  121.0 3.6 %collective-permute-done.3 = bf16[1,64,4,256]{1,3,2,0:T(8,128)(2,1)} collective-permute-done((bf16[1,64,4,256]{1,3,2,0:T(8,128)(2,1)}, bf16[1,64,4,256]{1,3,2,0:T(8,128)(2,1)}, u32[]{:S(2)}, u32[]{:S(2)}) %collective-permute-start.3) | collective-permute-done | bytes 131104 | tf_op jit(solution)/shard_map/ppermute | solution.py:25
  124.6 3.2 %select_maximum_fusion = bf16[64,16,24,24]{0,3,2,1:T(8,128)(2,1)S(1)} fusion(bf16[64,4,16,16]{0,3,2,1:T(8,128)(2,1)} %bitcast.37, bf16[64,8,16,16]{0,3,2,1:T(8,128)(2,1)S(1)} %bitcast.148, bf16[64,4,16,16]{0,3,2,1:T(8,128)(2,1)} %bitcast.35), kind=kLoop, calls=%fused_computation.59 | loop fusion | flops 11206656 | bytes 1703936 | tf_op jit(solution)/shard_map/concatenate | solution.py:26
  127.9 7.0 %constant_dynamic-slice_fusion.9 = (bf16[64,8,16,16]{0,3,2,1:T(8,128)(2,1)}, bf16[64,8,16,16]{0,3,2,1:T(8,128)(2,1)S(1)}, bf16[64,8,16,16]{0,3,2,1:T(8,128)(2,1)...) fusion(bf16[64,16,24,24]{0,3,2,1:T(8,128)(2,1)S(1)} %select_max, ...), kind=kLoop, calls=%fused_computation.120 | loop fusion | bytes 13631504 | tf_op jit(solution)/shard_map/dynamic_slice | solution.py:48
  158.0 5.3 %concatenate.63 = bf16[576,2048]{0,1:T(8,128)(2,1)S(1)} concatenate(bf16[64,2048]{0,1:T(8,128)(2,1)} %bitcast.186, bf16[64,2048]{0,1:T(8,128)(2,1)} %bitcast.185, bf16[64,2048]{0,1:T(8,128)(2,1)} %bitcast.184, bf16[64,2048]{0,1:T(8,128)(2,1)} %bitcast.183, bf16[64,2048]{0,1:T(8,128)(2,1)} %bitcast.182, bf16[64,2048]{0,1:T(8,128)(2,1)} %bitcast.181, bf16[64,2048]{0,1:T(8,128)(2,1)} %bitcast.180, ...), dimensions={0} | concatenate | bytes 4718592 | tf_op jit(solution)/shard_map/concatenate | solution.py:50
  164.8 5.2 %concatenate.65 = bf16[576,2048]{0,1:T(8,128)(2,1)S(1)} concatenate(bf16[64,2048]{0,1:T(8,128)(2,1)} %bitcast.176, bf16[64,2048]{0,1:T(8,128)(2,1)} %bitcast.175, bf16[64,2048]{0,1:T(8,128)(2,1)} %bitcast.174, bf16[64,2048]{0,1:T(8,128)(2,1)} %bitcast.173, bf16[64,2048]{0,1:T(8,128)(2,1)} %bitcast.172, bf16[64,2048]{0,1:T(8,128)(2,1)} %bitcast.171, bf16[64,2048]{0,1:T(8,128)(2,1)} %bitcast.170, ...), dimensions={0} | concatenate | bytes 4718592 | tf_op jit(solution)/shard_map/concatenate | solution.py:50
  175.2 19.8 %all-reduce.3 = (f32[64]{0:T(128)S(1)}, f32[64]{0:T(128)S(1)}) all-reduce(f32[64]{0:T(128)S(1)} %broadcast_multiply_fusion.3, f32[64]{0:T(128)S(1)} %broadcast_multiply_fusion.2), channel_id=1, replica_groups=mesh['wrap'=8,'samp'=4] {'wrap'}, use_global_device_ids=true, to_apply=%region_3.4 | all-reduce | flops 128 | bytes 1024 | tf_op jit(solution)/shard_map/psum | solution.py:13
  195.0 6.2 %all-reduce.5 = (f32[64]{0:T(128)}, f32[64]{0:T(128)}) all-reduce(f32[64]{0:T(128)S(1)} %get-tuple-element.5, f32[64]{0:T(128)S(1)} %get-tuple-element.6), channel_id=1, replica_groups=mesh['wrap'=8,'samp'=4] {'samp'}, use_global_device_ids=true, to_apply=%region_4.5 | all-reduce | flops 128 | bytes 1024 | tf_op jit(solution)/shard_map/psum | solution.py:14
  203.8 47.0 %all-reduce.10.cloned.1.call-done = (f32[64,1728]{1,0:T(8,128)}, f32[64,1728]{1,0:T(8,128)}) async-done(((f32[64,1728]{1,0:T(8,128)}, f32[64,1728]{1,0:T(8,128)}), (f32[64,1728]{1,0:T(8,128)}, f32[64,1728]{1,0:T(8,128)})) %all-reduce.10.cloned.1.call-update) | async-done | bytes 884752 | tf_op jit(solution)/shard_map/psum | solution.py:13
  253.9 34.0 %all-reduce.12.cloned.1.call-done = (f32[64,1728]{1,0:T(8,128)}, f32[64,1728]{1,0:T(8,128)}) async-done(((f32[64,1728]{1,0:T(8,128)}, f32[64,1728]{1,0:T(8,128)}), (f32[64,1728]{1,0:T(8,128)}, f32[64,1728]{1,0:T(8,128)})) %all-reduce.12.cloned.1.call-update) | async-done | bytes 884752 | tf_op jit(solution)/shard_map/psum | solution.py:14
  (95 shorter events, 73.1 us)
Async XLA Ops:
  7.2 14.4 %copy-start.12 = (s32[2]{0:T(128)S(1)}, s32[2]{0:T(128)}, u32[]{:S(2)}) copy-start(s32[2]{0:T(128)} %param.13) | copy-start | bytes 28
  7.2 20.2 %copy-start.10 = (bf16[64,1728]{1,0:T(8,128)(2,1)S(1)}, bf16[64,1728]{1,0:T(8,128)(2,1)}, u32[]{:S(2)}) copy-start(bf16[64,1728]{1,0:T(8,128)(2,1)} %param.11) | copy-start | bytes 663556
  7.2 243.7 %all-reduce.10.cloned.1.call-start = ((), (), s32[]{:S(2)}) async-start(), calls=%async_computation | async-start | bytes 1835008 | tf_op jit(solution)/shard_map/psum | solution.py:13
  8.6 22.0 %collective-permute-start.4 = (bf16[1,64,4,256]{1,3,2,0:T(8,128)(2,1)S(1)}, bf16[1,64,4,256]{1,3,2,0:T(8,128)(2,1)}, u32[]{:S(2)}, u32[]{:S(2)}) collective-permute-start(bf16[1,64,4,256]{1,3,2,0:T(8,128)(2,1)S(1)} %get-tuple-element.93), channel_id=1, source_target_pairs={{0,4},{4,8},{8,12},{12,16},{16,20},{20,24},{24,28},{28,0},{1,5},{5... | collective-permute-start | bytes 393224 | tf_op jit(solution)/shard_map/ppermute | solution.py:24
  11.7 20.5 %collective-permute-start.5 = (bf16[1,64,4,256]{1,3,2,0:T(8,128)(2,1)S(1)}, bf16[1,64,4,256]{1,3,2,0:T(8,128)(2,1)}, u32[]{:S(2)}, u32[]{:S(2)}) collective-permute-start(bf16[1,64,4,256]{1,3,2,0:T(8,128)(2,1)S(1)} %get-tuple-element.94), channel_id=1, source_target_pairs={{4,0},{8,4},{12,8},{16,12},{20,16},{24,20},{28,24},{0,28},{5,1},{9... | collective-permute-start | bytes 393224 | tf_op jit(solution)/shard_map/ppermute | solution.py:25
  16.0 14.6 %copy-start.6 = (bf16[1,64,8,256]{3,2,1,0:T(8,128)(2,1)S(1)}, bf16[1,64,8,256]{3,2,1,0:T(8,128)(2,1)}, u32[]{:S(2)}) copy-start(bf16[1,64,8,256]{3,2,1,0:T(8,128)(2,1)} %param.8) | copy-start | bytes 786436
  16.9 25.7 %collective-permute-start = (bf16[1,64,4,256]{1,3,2,0:T(8,128)(2,1)}, bf16[1,64,4,256]{1,3,2,0:T(8,128)(2,1)}, u32[]{:S(2)}, u32[]{:S(2)}) collective-permute-start(bf16[1,64,4,256]{1,3,2,0:T(8,128)(2,1)} %get-tuple-element.97), channel_id=1, source_target_pairs={{0,4},{4,8},{8,12},{12,16},{16,20},{20,24},{24,28},{28,0},{1,5},{5... | collective-permute-start | bytes 393224 | tf_op jit(solution)/shard_map/ppermute | solution.py:24
  16.9 25.7 %collective-permute-start.1 = (bf16[1,64,4,256]{1,3,2,0:T(8,128)(2,1)}, bf16[1,64,4,256]{1,3,2,0:T(8,128)(2,1)}, u32[]{:S(2)}, u32[]{:S(2)}) collective-permute-start(bf16[1,64,4,256]{1,3,2,0:T(8,128)(2,1)} %get-tuple-element.98), channel_id=1, source_target_pairs={{4,0},{8,4},{12,8},{16,12},{20,16},{24,20},{28,24},{0,28},{5,1},{9... | collective-permute-start | bytes 393224 | tf_op jit(solution)/shard_map/ppermute | solution.py:25
  85.6 6.8 %copy-start.14 = (f32[64]{0:T(128)S(1)}, f32[64]{0:T(128)}, u32[]{:S(2)}) copy-start(f32[64]{0:T(128)} %param.10) | copy-start | bytes 772
  92.4 3.7 %copy-start.8 = (bf16[64,8,16,16]{0,3,2,1:T(8,128)(2,1)S(1)}, bf16[64,8,16,16]{0,3,2,1:T(8,128)(2,1)}, u32[]{:S(2)}) copy-start(bf16[64,8,16,16]{0,3,2,1:T(8,128)(2,1)} %get-tuple-element.39) | copy-start | bytes 786436
  102.8 3.2 %copy-start.4 = (bf16[576,2048]{0,1:T(8,128)(2,1)S(1)}, bf16[576,2048]{0,1:T(8,128)(2,1)}, u32[]{:S(2)}) copy-start(bf16[576,2048]{0,1:T(8,128)(2,1)} %concatenate.58) | copy-start | bytes 7077892
  106.0 3.1 %copy-start.5 = (bf16[64,2048]{1,0:T(8,128)(2,1)}, bf16[64,2048]{1,0:T(8,128)(2,1)S(1)}, u32[]{:S(2)}) copy-start(bf16[64,2048]{1,0:T(8,128)(2,1)S(1)} %get-tuple-element.104) | copy-start | bytes 786436
  106.1 1.9 copy-start.1
  111.2 9.8 %collective-permute-start.2 = (bf16[1,64,4,256]{1,3,2,0:T(8,128)(2,1)}, bf16[1,64,4,256]{1,3,2,0:T(8,128)(2,1)}, u32[]{:S(2)}, u32[]{:S(2)}) collective-permute-start(bf16[1,64,4,256]{1,3,2,0:T(8,128)(2,1)} %get-tuple-element.95), channel_id=1, source_target_pairs={{0,4},{4,8},{8,12},{12,16},{16,20},{20,24},{24,28},{28,0},{1,5},{5... | collective-permute-start | bytes 393224 | tf_op jit(solution)/shard_map/ppermute | solution.py:24
  111.2 13.4 %collective-permute-start.3 = (bf16[1,64,4,256]{1,3,2,0:T(8,128)(2,1)}, bf16[1,64,4,256]{1,3,2,0:T(8,128)(2,1)}, u32[]{:S(2)}, u32[]{:S(2)}) collective-permute-start(bf16[1,64,4,256]{1,3,2,0:T(8,128)(2,1)} %get-tuple-element.96), channel_id=1, source_target_pairs={{4,0},{8,4},{12,8},{16,12},{20,16},{24,20},{28,24},{0,28},{5,1},{9... | collective-permute-start | bytes 393224 | tf_op jit(solution)/shard_map/ppermute | solution.py:25
  136.8 9.7 %copy-start.9 = (bf16[64,2048]{1,0:T(8,128)(2,1)S(1)}, bf16[64,2048]{1,0:T(8,128)(2,1)}, u32[]{:S(2)}) copy-start(bf16[64,2048]{1,0:T(8,128)(2,1)} %get-tuple-element.101) | copy-start | bytes 786436
  156.5 1.5 copy-start.2
  163.3 1.5 copy-start
  171.3 3.3 %copy-start.7 = (bf16[1,64,8,256]{3,2,1,0:T(8,128)(2,1)S(1)}, bf16[1,64,8,256]{3,2,1,0:T(8,128)(2,1)}, u32[]{:S(2)}) copy-start(bf16[1,64,8,256]{3,2,1,0:T(8,128)(2,1)} %param.8) | copy-start | bytes 786436
  174.6 113.4 %all-reduce.12.cloned.1.call-start = ((), (), s32[]{:S(2)}) async-start(), calls=%async_computation.1 | async-start | bytes 1835008 | tf_op jit(solution)/shard_map/psum | solution.py:14
  201.1 49.7 %copy-start.11 = (bf16[64,1728]{1,0:T(8,128)(2,1)S(1)}, bf16[64,1728]{1,0:T(8,128)(2,1)}, u32[]{:S(2)}) copy-start(bf16[64,1728]{1,0:T(8,128)(2,1)} %param.11) | copy-start | bytes 663556
  250.9 1.7 copy-start.3
  250.9 1.7 copy-start.13
Sparse Core Ops, SparseCore 0:
  174.7 76.1 all-reduce.9
  253.2 34.6 all-reduce.11
